TPU v7x, 32 devices: a whole 2x2x4 slice. The times are simulated.
32 devices in a mesh: ctx: 16 (over z, y, core), fsdp: 2 (over x).
Axes of the slice: x: 2, y: 2, z: 4, core: 2. Of those that a mesh axis runs over, the one named last changes fastest.
Arguments:
- queries: bfloat16 [2, 2048, 2048], P('fsdp', 'ctx'), may hold values from -8 to 8
- keys_values: bfloat16 [2, 2048, 2, 2048], P('fsdp', 'ctx'), may hold values from -8 to 8
- upstream: bfloat16 [2, 2048, 2048], P('fsdp', 'ctx'), may hold values from -6 to 6
- out_weight: bfloat16 [2048, 2048], P('fsdp'), may hold values from -0.125 to 0.125
Outputs:
- grad_queries: bfloat16 [2, 2048, 2048], P('fsdp', 'ctx')
- grad_keys_values: bfloat16 [2, 2048, 2, 2048], P('fsdp', 'ctx')
- grad_weight: float32 [2048, 2048], P(('ctx', 'fsdp'))
All inputs are finite; a program needn't handle non-finite values.
Results may differ from a plain program's by a relative error of at most 0.014.
Values may be sent and summed in bfloat16 or wider, within the bound.
A program may use at most 128 MiB of HBM per device.

v0:
```python
import jax
import jax.numpy as jnp
from jax import lax
from jax.sharding import PartitionSpec as P

HEADS = 16
HEAD_DIM = 128
SPAN = 4
WINDOW = 512


NEGATIVE = -1e30


def passed_along(x, axis, by):
    count = lax.axis_size(axis)
    pairs = [(i, i + by) for i in range(count) if 0 <= i + by < count]
    return lax.ppermute(x, axis, pairs)


def shards(queries, keys_values, upstream, out_weight):
    seq_count, tok_rows, attn_width = queries.shape
    model_width = upstream.shape[2]
    head_count = HEADS
    head_size = HEAD_DIM
    reach_devices = SPAN
    inv_root = head_size ** (-0.5)
    flat_upstream = upstream.reshape(seq_count * tok_rows, model_width)
    grad_attn = jnp.dot(
        flat_upstream,
        lax.all_gather(out_weight, "fsdp", axis=0, tiled=True),
        preferred_element_type=jnp.float32,
    )
    grad_attn = grad_attn.astype(jnp.bfloat16).reshape(seq_count, tok_rows, head_count, head_size)
    moving = keys_values
    earlier = []
    for offset in range(reach_devices):
        moving = passed_along(moving, "ctx", 1)
        earlier = [moving] + earlier
    window_kv = jnp.concatenate(earlier + [keys_values], axis=1)
    key_count = window_kv.shape[1]
    key_heads = window_kv[:, :, 0].reshape(seq_count, key_count, head_count, head_size)
    value_heads = window_kv[:, :, 1].reshape(seq_count, key_count, head_count, head_size)
    query_heads = queries.reshape(seq_count, tok_rows, head_count, head_size)
    ctx_index = lax.axis_index("ctx")
    query_pos = ctx_index * tok_rows + jnp.arange(tok_rows, dtype=jnp.int32)
    key_pos = (ctx_index - reach_devices) * tok_rows + jnp.arange(key_count, dtype=jnp.int32)
    distance = query_pos[:, None] - key_pos[None, :]
    visible = (distance >= 0) & (distance < WINDOW) & (key_pos[None, :] >= 0)
    scores = (
        jnp.einsum("sqhe,skhe->shqk", query_heads, key_heads, preferred_element_type=jnp.float32)
        * inv_root
    )
    scores = jnp.where(visible[None, None], scores, NEGATIVE)
    row_max = jnp.max(scores, axis=-1, keepdims=True)
    lifted = jnp.exp(scores - row_max)
    probability = lifted / jnp.sum(lifted, axis=-1, keepdims=True)
    probs_low = probability.astype(jnp.bfloat16)
    attended = jnp.einsum(
        "shqk,skhe->sqhe", probs_low, value_heads, preferred_element_type=jnp.float32
    ).astype(jnp.bfloat16)
    products = jnp.einsum(
        "sqhe,skhe->shqk", grad_attn, value_heads, preferred_element_type=jnp.float32
    )
    center = jnp.sum(grad_attn.astype(jnp.float32) * attended.astype(jnp.float32), axis=-1)
    center = jnp.swapaxes(center, 1, 2)[:, :, :, None]
    grad_scores = (probability * (products - center)).astype(jnp.bfloat16)
    grad_queries = (
        jnp.einsum("shqk,skhe->sqhe", grad_scores, key_heads, preferred_element_type=jnp.float32)
        * inv_root
    )
    grad_queries = grad_queries.astype(jnp.bfloat16).reshape(seq_count, tok_rows, attn_width)
    grad_keys = (
        jnp.einsum("shqk,sqhe->skhe", grad_scores, query_heads, preferred_element_type=jnp.float32)
        * inv_root
    )
    grad_values = jnp.einsum(
        "shqk,sqhe->skhe", probs_low, grad_attn, preferred_element_type=jnp.float32
    )
    grad_window = jnp.stack(
        [
            grad_keys.reshape(seq_count, key_count, attn_width),
            grad_values.reshape(seq_count, key_count, attn_width),
        ],
        axis=2,
    )
    blocks = [
        grad_window[:, offset * tok_rows : (offset + 1) * tok_rows]
        for offset in range(reach_devices + 1)
    ]
    carried = blocks[0]
    for offset in range(1, reach_devices + 1):
        carried = passed_along(carried, "ctx", -1)
        if offset < reach_devices:
            carried = carried + blocks[offset]
    collected = blocks[reach_devices] + carried
    grad_pairs = collected.astype(jnp.bfloat16)
    flat_attended = attended.reshape(seq_count * tok_rows, attn_width)
    weight_term = lax.dot_general(
        flat_upstream, flat_attended, (((0,), (0,)), ((), ())), preferred_element_type=jnp.float32
    )
    weight_term = lax.optimization_barrier(weight_term.astype(jnp.bfloat16)).astype(jnp.float32)
    ctx_count = lax.axis_size("ctx")
    fsdp_count = lax.axis_size("fsdp")
    own_rows = model_width // (ctx_count * fsdp_count)
    weight_term = weight_term.reshape(ctx_count, fsdp_count, own_rows, attn_width)
    section_one = lax.psum_scatter(weight_term, "ctx", scatter_dimension=0, tiled=True)
    section_two = lax.psum_scatter(section_one, "fsdp", scatter_dimension=1, tiled=True)
    grad_weight = section_two.reshape(own_rows, attn_width)
    return (grad_queries, grad_pairs, grad_weight)


def solution(mesh):
    return jax.shard_map(
        shards,
        mesh=mesh,
        in_specs=(
            P("fsdp", "ctx", None),
            P("fsdp", "ctx", None, None),
            P("fsdp", "ctx", None),
            P("fsdp", None),
        ),
        out_specs=(P("fsdp", "ctx", None), P("fsdp", "ctx", None, None), P(("ctx", "fsdp"), None)),
        check_vma=False,
    )
```

profile of v0, /device:TPU:0, one launch (start us, length us, event | category | flops | bytes accessed | tf_op | source)
XLA Modules:
  0.0 428.0 jit_solution(18424261364848707581)
XLA Ops:
  8.0 2.5 copy.23
  10.5 2.5 collective-permute-start
  15.2 14.0 %collective-permute-start.1 = (bf16[1,128,2,2048]{1,3,2,0:T(8,128)(2,1)S(1)}, bf16[1,128,2,2048]{1,3,2,0:T(8,128)(2,1)S(1)}, u32[]{:S(2)}, u32[]{:S(2)}) collective-permute-start(bf16[1,128,2,2048]{1,3,2,0:T(8,128)(2,1)S(1)} %collective-permute-done), channel_id=1, source_target_pairs={{0,2},{2,4},{4,6},{6,8},{8,10},{10,12},{12,14},{14,16},{16,18},{18... | collective-permute-start | bytes 3145736 | tf_op jit(solution)/shard_map/ppermute | solution.py:18
  32.4 14.8 %collective-permute-start.2 = (bf16[1,128,2,2048]{1,3,2,0:T(8,128)(2,1)S(1)}, bf16[1,128,2,2048]{1,3,2,0:T(8,128)(2,1)}, u32[]{:S(2)}, u32[]{:S(2)}) collective-permute-start(bf16[1,128,2,2048]{1,3,2,0:T(8,128)(2,1)S(1)} %collective-permute-done.1), channel_id=1, source_target_pairs={{0,2},{2,4},{4,6},{6,8},{8,10},{10,12},{12,14},{14,16},{16,18},{18... | collective-permute-start | bytes 3145736 | tf_op jit(solution)/shard_map/ppermute | solution.py:18
  48.7 14.7 %collective-permute-start.3 = (bf16[1,128,2,2048]{1,3,2,0:T(8,128)(2,1)}, bf16[1,128,2,2048]{1,3,2,0:T(8,128)(2,1)}, u32[]{:S(2)}, u32[]{:S(2)}) collective-permute-start(bf16[1,128,2,2048]{1,3,2,0:T(8,128)(2,1)} %collective-permute-done.2), channel_id=1, source_target_pairs={{0,2},{2,4},{4,6},{6,8},{8,10},{10,12},{12,14},{14,16},{16,18},{18... | collective-permute-start | bytes 3145736 | tf_op jit(solution)/shard_map/ppermute | solution.py:18
  71.8 5.8 %fusion.25 = (f32[16,128]{1,0:T(8,128)S(1)}, f32[16,128,640]{1,2,0:T(8,128)}) fusion(pred[128,640]{0,1:T(8,128)(4,1)S(1)} %fusion.19, bf16[640,16,128]{0,2,1:T(8,128)(2,1)S(1)} %bitcast.80, bf16[128,16,128]{0,2,1:T(8,128)(2,1)} %bitcast.86), kind=kOutput, calls=%fused_computation.53 | convolution fusion | flops 340787840 | bytes 8478720 | tf_op jit(solution)/shard_map/sub | solution.py:56
  77.6 3.1 fusion.5
  80.8 35.5 %all-gather.2.cloned.1.call-done = bf16[2048,2048]{1,0:T(8,128)(2,1)} async-done(((bf16[1024,2048]{1,0:T(8,128)(2,1)}), bf16[2048,2048]{1,0:T(8,128)(2,1)}) %all-gather.2.cloned.1.call-update) | async-done | bytes 8388624 | tf_op jit(solution)/shard_map/all_gather | solution.py:31
  116.3 5.5 %convolution_convert_fusion = bf16[128,2048]{1,0:T(8,128)(2,1)} fusion(bf16[2048,2048]{1,0:T(8,128)(2,1)} %all-gather.2.cloned.1.call-done, bf16[1,128,2048]{2,1,0:T(8,128)(2,1)S(1)} %copy-done), kind=kOutput, calls=%fused_computation.19 | convolution fusion | flops 1074003968 | bytes 9437184 | tf_op jit(solution)/shard_map/dot_general | solution.py:29
  121.8 2.2 copy.50
  124.0 2.9 multiply_reduce_fusion
  126.8 5.6 %convert_bitcast_fusion = bf16[2048,2048]{0,1:T(8,128)(2,1)} fusion(bf16[128,2048]{0,1:T(8,128)(2,1)S(1)} %bitcast.85, bf16[1,128,2048]{2,1,0:T(8,128)(2,1)S(1)} %copy-done), kind=kOutput, calls=%fused_computation.9 | convolution fusion | flops 1077936128 | bytes 9437184 | tf_op jit(solution)/shard_map/dot_general | solution.py:99
  132.5 13.0 %copy.39 = f32[2048,2048]{1,0:T(8,128)} copy(bf16[2048,2048]{0,1:T(8,128)(2,1)} %convert_bitcast_fusion) | data formatting | bytes 25165824 | tf_op jit(solution)/shard_map/reshape | solution.py:106
  147.5 4.8 %multiply_convert_fusion = bf16[16,128,640]{1,2,0:T(8,128)(2,1)S(1)} fusion(f32[16,128]{1,0:T(8,128)S(1)} %bitcast.91, bf16[128,16,128]{0,2,1:T(8,128)(2,1)} %bitcast.88, bf16[640,16,128]{0,2,1:T(8,128)(2,1)} %bitcast.83, f32[16,128,640]{1,2,0:T(8,128)} %get-tuple-element.12, f32[16,128]{1,0:T(8,128)S(1)} %get-tuple-element.11), kind=kOutput, calls=%fused_computation.12 | convolution fusion | flops 340787200 | bytes 11026432 | tf_op jit(solution)/shard_map/sqhe,skhe->shqk/dot_general | solution.py:62
  153.8 3.7 multiply_bitcast_fusion
  157.5 6.7 %copy.36 = f32[1,640,16,128]{1,3,2,0:T(8,128)} copy(f32[1,640,16,128]{3,1,2,0:T(8,128)} %multiply_bitcast_fusion) | data formatting | bytes 10485760 | tf_op jit(solution)/shard_map/mul | solution.py:74
  165.2 4.2 copy-done.2
  170.9 4.8 %collective-permute-done.4 = f32[1,128,2,2048]{1,3,2,0:T(8,128)S(1)} collective-permute-done((f32[1,128,2,2048]{1,3,2,0:T(8,128)S(1)}, f32[1,128,2,2048]{1,3,2,0:T(8,128)S(1)}, u32[]{:S(2)}, u32[]{:S(2)}) %collective-permute-start.4) | collective-permute-done | bytes 2097184 | tf_op jit(solution)/shard_map/ppermute | solution.py:18
  177.3 36.9 %collective-permute-done.5 = f32[1,128,2,2048]{1,3,2,0:T(8,128)S(1)} collective-permute-done((f32[1,128,2,2048]{1,3,2,0:T(8,128)S(1)}, f32[1,128,2,2048]{1,3,2,0:T(8,128)S(1)}, u32[]{:S(2)}, u32[]{:S(2)}) %collective-permute-start.5) | collective-permute-done | bytes 2097184 | tf_op jit(solution)/shard_map/ppermute | solution.py:18
  216.1 37.7 %collective-permute-done.6 = f32[1,128,2,2048]{1,3,2,0:T(8,128)S(1)} collective-permute-done((f32[1,128,2,2048]{1,3,2,0:T(8,128)S(1)}, f32[1,128,2,2048]{1,3,2,0:T(8,128)S(1)}, u32[]{:S(2)}, u32[]{:S(2)}) %collective-permute-start.6) | collective-permute-done | bytes 2097184 | tf_op jit(solution)/shard_map/ppermute | solution.py:18
  256.6 142.5 %reduce-scatter.3.cloned.1.call-done = f32[1,2,64,2048]{3,2,1,0:T(8,128)} async-done(((f32[16,2,64,2048]{3,2,1,0:T(8,128)}), f32[1,2,64,2048]{3,2,1,0:T(8,128)}) %reduce-scatter.3.cloned.1.call-update) | async-done | bytes 1048592 | tf_op jit(solution)/shard_map/reduce_scatter | solution.py:107
  399.2 3.4 fusion.15
  404.7 2.4 fusion.10
  409.1 12.4 %reduce-scatter.5.cloned.1.call-done = f32[1,1,64,2048]{3,2,1,0:T(8,128)} async-done(((f32[1,2,64,2048]{3,2,1,0:T(8,128)}), f32[1,1,64,2048]{3,2,1,0:T(8,128)}) %reduce-scatter.5.cloned.1.call-update) | async-done | bytes 524304 | tf_op jit(solution)/shard_map/reduce_scatter | solution.py:108
  (57 shorter events, 32.4 us)
Async XLA Ops:
  7.2 109.1 %copy-start = (bf16[1,128,2048]{2,1,0:T(8,128)(2,1)S(1)}, bf16[1,128,2048]{2,1,0:T(8,128)(2,1)}, u32[]{:S(2)}) copy-start(bf16[1,128,2048]{2,1,0:T(8,128)(2,1)} %param.6) | copy-start | bytes 1572868
  7.2 56.2 %copy-start.11 = (bf16[1,128,2048]{2,1,0:T(8,128)(2,1)S(1)}, bf16[1,128,2048]{2,1,0:T(8,128)(2,1)}, u32[]{:S(2)}) copy-start(bf16[1,128,2048]{2,1,0:T(8,128)(2,1)} %param.4) | copy-start | bytes 1572868
  7.2 109.1 %all-gather.2.cloned.1.call-start = ((), (), s32[]{:S(2)}) async-start(), calls=%async_computation.2 | async-start | bytes 12582912 | tf_op jit(solution)/shard_map/all_gather | solution.py:31
  7.9 391.2 %reduce-scatter.3.cloned.1.call-start = ((), (), s32[]{:S(2)}) async-start(), calls=%async_computation.3 | async-start | bytes 17825792 | tf_op jit(solution)/shard_map/reduce_scatter | solution.py:107
  10.5 4.7 %collective-permute-start = (bf16[1,128,2,2048]{1,3,2,0:T(8,128)(2,1)S(1)}, bf16[1,128,2,2048]{1,3,2,0:T(8,128)(2,1)S(1)}, u32[]{:S(2)}, u32[]{:S(2)}) collective-permute-start(bf16[1,128,2,2048]{1,3,2,0:T(8,128)(2,1)S(1)} %copy.23), channel_id=1, source_target_pairs={{0,2},{2,4},{4,6},{6,8},{8,10},{10,12},{12,14},{14,16},{16,18},{18... | collective-permute-start | bytes 3145736 | tf_op jit(solution)/shard_map/ppermute | solution.py:18
  15.2 16.2 %collective-permute-start.1 = (bf16[1,128,2,2048]{1,3,2,0:T(8,128)(2,1)S(1)}, bf16[1,128,2,2048]{1,3,2,0:T(8,128)(2,1)S(1)}, u32[]{:S(2)}, u32[]{:S(2)}) collective-permute-start(bf16[1,128,2,2048]{1,3,2,0:T(8,128)(2,1)S(1)} %collective-permute-done), channel_id=1, source_target_pairs={{0,2},{2,4},{4,6},{6,8},{8,10},{10,12},{12,14},{14,16},{16,18},{18... | collective-permute-start | bytes 3145736 | tf_op jit(solution)/shard_map/ppermute | solution.py:18
  31.4 1.0 copy-start.10
  32.4 16.2 %collective-permute-start.2 = (bf16[1,128,2,2048]{1,3,2,0:T(8,128)(2,1)S(1)}, bf16[1,128,2,2048]{1,3,2,0:T(8,128)(2,1)}, u32[]{:S(2)}, u32[]{:S(2)}) collective-permute-start(bf16[1,128,2,2048]{1,3,2,0:T(8,128)(2,1)S(1)} %collective-permute-done.1), channel_id=1, source_target_pairs={{0,2},{2,4},{4,6},{6,8},{8,10},{10,12},{12,14},{14,16},{16,18},{18... | collective-permute-start | bytes 3145736 | tf_op jit(solution)/shard_map/ppermute | solution.py:18
  48.7 16.3 %collective-permute-start.3 = (bf16[1,128,2,2048]{1,3,2,0:T(8,128)(2,1)}, bf16[1,128,2,2048]{1,3,2,0:T(8,128)(2,1)}, u32[]{:S(2)}, u32[]{:S(2)}) collective-permute-start(bf16[1,128,2,2048]{1,3,2,0:T(8,128)(2,1)} %collective-permute-done.2), channel_id=1, source_target_pairs={{0,2},{2,4},{4,6},{6,8},{8,10},{10,12},{12,14},{14,16},{16,18},{18... | collective-permute-start | bytes 3145736 | tf_op jit(solution)/shard_map/ppermute | solution.py:18
  71.8 5.8 %copy-start.4 = (bf16[1,640,1,2048]{1,3,2,0:T(8,128)(2,1)}, bf16[1,640,1,2048]{1,3,2,0:T(8,128)(2,1)S(1)}, u32[]{:S(2)}) copy-start(bf16[1,640,1,2048]{1,3,2,0:T(8,128)(2,1)S(1)} %get-tuple-element.10) | copy-start | bytes 7864324
  145.5 1.0 copy-start.7
  145.5 276.0 %reduce-scatter.5.cloned.1.call-start = ((), (), s32[]{:S(2)}) async-start(), calls=%async_computation.4 | async-start | bytes 1572864 | tf_op jit(solution)/shard_map/reduce_scatter | solution.py:108
  147.5 6.3 %copy-start.8 = (bf16[1,128,2048]{1,2,0:T(8,128)(2,1)S(1)}, bf16[1,128,2048]{1,2,0:T(8,128)(2,1)}, u32[]{:S(2)}) copy-start(bf16[1,128,2048]{1,2,0:T(8,128)(2,1)} %copy.51) | copy-start | bytes 1572868
  152.3 1.5 copy-start.6
  157.5 6.7 %copy-start.9 = (bf16[128,2048]{0,1:T(8,128)(2,1)S(1)}, bf16[128,2048]{0,1:T(8,128)(2,1)}, u32[]{:S(2)}) copy-start(bf16[128,2048]{0,1:T(8,128)(2,1)} %copy.52) | copy-start | bytes 1572868
  164.2 5.3 %copy-start.2 = (f32[1,640,16,128]{1,3,2,0:T(8,128)S(1)}, f32[1,640,16,128]{1,3,2,0:T(8,128)}, u32[]{:S(2)}) copy-start(f32[1,640,16,128]{1,3,2,0:T(8,128)} %copy.36) | copy-start | bytes 15728644
  165.2 88.5 %copy-start.3 = (f32[16,128,640]{2,1,0:T(8,128)}, f32[16,128,640]{2,1,0:T(8,128)S(1)}, u32[]{:S(2)}) copy-start(f32[16,128,640]{2,1,0:T(8,128)S(1)} %fusion.26) | copy-start | bytes 15728644
  169.6 6.1 %collective-permute-start.4 = (f32[1,128,2,2048]{1,3,2,0:T(8,128)S(1)}, f32[1,128,2,2048]{1,3,2,0:T(8,128)S(1)}, u32[]{:S(2)}, u32[]{:S(2)}) collective-permute-start(f32[1,128,2,2048]{1,3,2,0:T(8,128)S(1)} %fusion.11), channel_id=1, source_target_pairs={{2,0},{4,2},{6,4},{8,6},{10,8},{12,10},{14,12},{16,14},{18,16},{20... | collective-permute-start | bytes 6291464 | tf_op jit(solution)/shard_map/ppermute | solution.py:18
  176.1 38.2 %collective-permute-start.5 = (f32[1,128,2,2048]{1,3,2,0:T(8,128)S(1)}, f32[1,128,2,2048]{1,3,2,0:T(8,128)S(1)}, u32[]{:S(2)}, u32[]{:S(2)}) collective-permute-start(f32[1,128,2,2048]{1,3,2,0:T(8,128)S(1)} %fusion.13), channel_id=1, source_target_pairs={{2,0},{4,2},{6,4},{8,6},{10,8},{12,10},{14,12},{16,14},{18,16},{20... | collective-permute-start | bytes 6291464 | tf_op jit(solution)/shard_map/ppermute | solution.py:18
  214.5 184.7 %copy-start.5 = (bf16[1,640,1,2048]{1,3,2,0:T(8,128)(2,1)S(1)}, bf16[1,640,1,2048]{1,3,2,0:T(8,128)(2,1)}, u32[]{:S(2)}) copy-start(bf16[1,640,1,2048]{1,3,2,0:T(8,128)(2,1)} %copy-done.4) | copy-start | bytes 7864324
  214.5 39.3 %collective-permute-start.6 = (f32[1,128,2,2048]{1,3,2,0:T(8,128)S(1)}, f32[1,128,2,2048]{1,3,2,0:T(8,128)S(1)}, u32[]{:S(2)}, u32[]{:S(2)}) collective-permute-start(f32[1,128,2,2048]{1,3,2,0:T(8,128)S(1)} %fusion.7), channel_id=1, source_target_pairs={{2,0},{4,2},{6,4},{8,6},{10,8},{12,10},{14,12},{16,14},{18,16},{20... | collective-permute-start | bytes 6291464 | tf_op jit(solution)/shard_map/ppermute | solution.py:18
  255.4 149.3 %collective-permute-start.7 = (f32[1,128,2,2048]{1,3,2,0:T(8,128)}, f32[1,128,2,2048]{1,3,2,0:T(8,128)}, u32[]{:S(2)}, u32[]{:S(2)}) collective-permute-start(f32[1,128,2,2048]{1,3,2,0:T(8,128)} %fusion.14), channel_id=1, source_target_pairs={{2,0},{4,2},{6,4},{8,6},{10,8},{12,10},{14,12},{16,14},{18,16},{20... | collective-permute-start | bytes 6291464 | tf_op jit(solution)/shard_map/ppermute | solution.py:18
  402.6 18.9 %copy-start.1 = (bf16[1,128,2048]{2,1,0:T(8,128)(2,1)S(1)}, bf16[1,128,2048]{2,1,0:T(8,128)(2,1)}, u32[]{:S(2)}) copy-start(bf16[1,128,2048]{2,1,0:T(8,128)(2,1)} %param.6) | copy-start | bytes 1572868
Sparse Core Ops, SparseCore 0:
  9.5 106.6 all-gather.1
  145.6 253.4 reduce-scatter.2
  402.0 19.4 reduce-scatter.4
where the time goes:
time: 429 us; the launch traced here: 428 us
  waiting for transfers between devices  277 us (65%)
  starting transfers between devices  51.7 us (12%)
  local copies, waits for them, and re-layouts  44.9 us (10%)
  matrix products  32.7 us (8%)
  between operations  13.9 us (3%)
  other arithmetic  8.09 us (2%)
    reduce_scatter x1, waiting for transfers between devices, shards(): lax.psum_scatter(weight_term, 'ctx', scatter_dimension=0, tiled=True)  143 us
    ppermute x8, waiting for transfers between devices, passed_along(): return lax.ppermute(x, axis, pairs)  85.5 us
    ppermute x8, starting transfers between devices, passed_along(): return lax.ppermute(x, axis, pairs)  51.4 us
    all_gather x1, waiting for transfers between devices, shards(): lax.all_gather(out_weight, 'fsdp', axis=0, tiled=True)  35.5 us
    unnamed x31, local copies, waits for them, and re-layouts  18.8 us
    reshape x1, local copies, waits for them, and re-layouts, shards(): weight_term.reshape(ctx_count, fsdp_count, own_rows, attn_width)  13 us
    reduce_scatter x1, waiting for transfers between devices, shards(): lax.psum_scatter(section_one, 'fsdp', scatter_dimension=1, tiled=True)  12.4 us
  transfers between devices with their start and end apart: 11, of which 10 were waited for; matrix products, arithmetic and copies ran while one was open for 11% of the time, Pallas kernels for 0%

commit v1 on v0

v1 whole, which is shorter than its diff:
```python
import functools

import jax
import jax.numpy as jnp
from jax import lax
from jax.experimental import pallas as pl
from jax.experimental.pallas import tpu as pltpu
from jax.sharding import PartitionSpec as P

HEADS = 16
HEAD_DIM = 128
SPAN = 4
WINDOW = 512
NEGATIVE = -1e30
CHUNKS = 8
F32 = jnp.float32
BF16 = jnp.bfloat16


class Place:
    def __init__(self, planes, fsdp):
        self.planes, self.fsdp = planes, fsdp
        me = lax.axis_index("ctx")
        self.f = lax.axis_index("fsdp")
        self.p = lax.div(me, SPAN)
        self.r = lax.rem(me, SPAN)
        self.core = lax.rem(self.r, 2)
        self.y = lax.div(self.r, 2)
        self.mate = self.r + 1 - 2 * self.core
        self.across = lax.rem(self.r + 2, SPAN)

    def dev(self, p, r, f):
        return {"ctx": p * SPAN + r, "fsdp": f}

    def members(self):
        for dr in range(SPAN):
            for df in range(self.fsdp):
                if dr or df:
                    yield lax.rem(self.r + dr, SPAN), lax.rem(self.f + df, self.fsdp), dr, df

    def barrier(self):
        sem = pltpu.get_barrier_semaphore()
        count = 0
        for r, f, _, _ in self.members():
            pl.semaphore_signal(sem, inc=1, device_id=self.dev(self.p, r, f), device_id_type=pl.DeviceIdType.MESH)
            count += 1
        for dp in range(1, self.planes):
            other = lax.rem(self.p + dp, self.planes)
            pl.semaphore_signal(sem, inc=1, device_id=self.dev(other, self.r, self.f), device_id_type=pl.DeviceIdType.MESH)
            count += 1
        pl.semaphore_wait(sem, count)


def remote(src, dst, send, recv, device):
    return pltpu.make_async_remote_copy(
        src_ref=src, dst_ref=dst, send_sem=send, recv_sem=recv, device_id=device, device_id_type=pl.DeviceIdType.MESH
    )


def chunk_of(ref, c, rows):
    per = CHUNKS // 2
    return ref.at[lax.div(c, per), pl.ds(pl.multiple_of(lax.rem(c, per) * rows, rows), rows)]


def gather_kernel(
    planes, fsdp,
    kv, up, up_cols, weight,
    win, grad_att, up_all,
    w_v, up_in, part_out, part_in, zeros,
    z_send, y_send, c_send, s_send, slot_recv, zero_sem, w_sem, u_send, u_recv, q_send, q_recv, m_send, m_recv, own_sem,
):
    at = Place(planes, fsdp)
    toks = up.shape[0]
    depth = weight.shape[0]
    width = weight.shape[1]
    rows = 2 * toks // CHUNKS
    f = at.f
    mine = at.r * fsdp + f
    w_copy = pltpu.make_async_copy(weight, w_v, w_sem)
    w_copy.start()
    zeros[...] = jnp.zeros_like(zeros)
    own_cols = pltpu.make_async_copy(up_cols.at[mine], up_all.at[mine], own_sem)
    own_cols.start()
    at.barrier()

    def up_copy(df):
        g = lax.rem(f + df, fsdp)
        return remote(
            up.at[:, pl.ds(pl.multiple_of(g * depth, 128), depth)], up_in.at[fsdp - df], u_send.at[df], u_recv.at[fsdp - df],
            at.dev(at.p, at.r, g),
        )

    def slot(j, c):
        return chunk_of(win.at[j], c, rows)

    def z_copy(c):
        return remote(chunk_of(kv, c, rows), slot(at.r, c), z_send.at[c], slot_recv.at[at.r, c], at.dev(at.p + 1, at.r, f))

    def y_copy(c, src):
        return remote(src, slot(at.r, c), y_send.at[c], slot_recv.at[at.r, c], at.dev(at.p, at.across, f))

    def c_copy(c, src):
        return remote(src, slot(at.r, c), c_send.at[c], slot_recv.at[at.r, c], at.dev(at.p, at.mate, f))

    def s_copy(c):
        return remote(slot(at.across, c), slot(at.across, c), s_send.at[c], slot_recv.at[at.across, c], at.dev(at.p, at.mate, f))

    def arrived(j, c):
        remote(slot(j, c), slot(j, c), z_send.at[c], slot_recv.at[j, c], at.dev(at.p, at.mate, f)).wait_recv()

    def zero_copy(c):
        return pltpu.make_async_copy(zeros, slot(at.r, c), zero_sem.at[c])

    for df in range(1, fsdp):
        up_copy(df).start()

    def begin(c, _):
        @pl.when(at.p < planes - 1)
        def _():
            z_copy(c).start()

        @pl.when(at.p == 0)
        def _():
            zero_copy(c).start()

        @pl.when(at.y == 0)
        def _():
            y_copy(c, chunk_of(kv, c, rows)).start()

        @pl.when(at.core == 0)
        def _():
            c_copy(c, chunk_of(kv, c, rows)).start()

        return 0

    lax.fori_loop(0, CHUNKS, begin, 0)

    def col_copy(r, g, dr, df):
        there = r * fsdp + g
        return remote(up_cols.at[there], up_all.at[mine], m_send.at[dr, df], m_recv.at[dr, df], at.dev(at.p, r, g))

    for r, g, dr, df in at.members():
        col_copy(r, g, dr, df).start()
    w_copy.wait()
    tile = 512

    def product(lhs_of, put):
        def step(t, _):
            cols = pl.ds(pl.multiple_of(t * tile, tile), tile)
            put(cols, jnp.dot(lhs_of(), w_v[:, cols], preferred_element_type=F32))
            return 0

        lax.fori_loop(0, width // tile, step, 0)

    def part_copy(df):
        return remote(
            part_out.at[df], part_in.at[fsdp - df], q_send.at[df], q_recv.at[fsdp - df],
            at.dev(at.p, at.r, lax.rem(f + df, fsdp)),
        )

    for df in range(1, fsdp):
        remote(up_in.at[df], up_in.at[df], u_send.at[df], u_recv.at[df], at.dev(at.p, at.r, lax.rem(f + df, fsdp))).wait_recv()

        def put(cols, value, df=df):
            part_out[df, :, cols] = value.astype(BF16)

        product(lambda df=df: up_in[df], put)
        part_copy(df).start()

    def forward(c, _):
        @pl.when(at.p == 0)
        def _():
            zero_copy(c).wait()

        @pl.when(at.p > 0)
        def _():
            arrived(at.r, c)

        @pl.when(at.y == 1)
        def _():
            y_copy(c, slot(at.r, c)).start()

        @pl.when(at.core == 1)
        def _():
            c_copy(c, slot(at.r, c)).start()

        return 0

    def share(c, _):
        arrived(at.across, c)
        s_copy(c).start()
        return 0

    def both(c, _):
        forward(c, 0)
        share(c, 0)
        return 0

    lax.fori_loop(0, CHUNKS, both, 0)
    own_depth = pl.ds(pl.multiple_of(f * depth, 128), depth)
    for df in range(1, fsdp):
        remote(part_in.at[df], part_in.at[df], q_send.at[df], q_recv.at[df], at.dev(at.p, at.r, lax.rem(f + df, fsdp))).wait_recv()

    def put_own(cols, value):
        for df in range(1, fsdp):
            value = value + part_in[df, :, cols].astype(F32)
        grad_att[:, cols] = value.astype(BF16)

    product(lambda: up[:, own_depth], put_own)

    def finish(c, _):
        arrived(at.mate, c)
        arrived(lax.rem(at.mate + 2, SPAN), c)

        @pl.when(at.p < planes - 1)
        def _():
            z_copy(c).wait_send()

        y_copy(c, slot(at.r, c)).wait_send()
        c_copy(c, slot(at.r, c)).wait_send()
        s_copy(c).wait_send()
        return 0

    lax.fori_loop(0, CHUNKS, finish, 0)
    for df in range(1, fsdp):
        up_copy(df).wait_send()
        part_copy(df).wait_send()
    own_cols.wait()
    for r, g, dr, df in at.members():
        col_copy(r, g, dr, df).wait_send()
        back = lax.rem(at.r + SPAN - dr, SPAN) * fsdp + lax.rem(f + fsdp - df, fsdp)
        remote(up_all.at[back], up_all.at[back], m_send.at[dr, df], m_recv.at[dr, df], at.dev(at.p, r, g)).wait_recv()


def attend_kernel(q_ref, kv_ref, win_ref, ga_ref, dq_ref, att_ref, dkv_ref, dwin_ref):
    me = lax.axis_index("ctx")
    toks = q_ref.shape[0]
    inv_root = HEAD_DIM ** (-0.5)
    r = lax.rem(me, SPAN)
    first_plane = lax.div(me, SPAN) == 0
    row = lax.broadcasted_iota(jnp.int32, (toks, toks), 0)
    col = lax.broadcasted_iota(jnp.int32, (toks, toks), 1)
    masks = []
    for j in range(SPAN):
        blocks = jnp.where(j < r, r - j, r - j + SPAN)
        distance = blocks * toks + row - col
        limit = jnp.where(jnp.logical_and(first_plane, j >= r), 0, WINDOW)
        masks.append((distance >= 0) & (distance < limit))
    masks.append((row - col >= 0) & (row - col < WINDOW))
    mask = jnp.concatenate(masks, axis=1)
    nt = (((1,), (1,)), ((), ()))
    tn = (((0,), (0,)), ((), ()))
    for h in range(q_ref.shape[1] // HEAD_DIM):
        cols = slice(h * HEAD_DIM, (h + 1) * HEAD_DIM)
        q = q_ref[:, cols]
        ga = ga_ref[:, cols]
        k = jnp.concatenate([win_ref[j, 0, :, cols] for j in range(SPAN)] + [kv_ref[0, :, cols]], axis=0)
        v = jnp.concatenate([win_ref[j, 1, :, cols] for j in range(SPAN)] + [kv_ref[1, :, cols]], axis=0)
        scores = lax.dot_general(q, k, nt, preferred_element_type=F32) * inv_root
        scores = jnp.where(mask, scores, NEGATIVE)
        lifted = jnp.exp(scores - jnp.max(scores, axis=-1, keepdims=True))
        prob = lifted * (1.0 / jnp.sum(lifted, axis=-1, keepdims=True))
        low = prob.astype(BF16)
        att = jnp.dot(low, v, preferred_element_type=F32).astype(BF16)
        att_ref[:, cols] = att
        products = lax.dot_general(ga, v, nt, preferred_element_type=F32)
        center = jnp.sum(ga.astype(F32) * att.astype(F32), axis=-1, keepdims=True)
        ds = (prob * (products - center)).astype(BF16)
        dq_ref[:, cols] = (jnp.dot(ds, k, preferred_element_type=F32) * inv_root).astype(BF16)
        dk = lax.dot_general(ds, q, tn, preferred_element_type=F32) * inv_root
        dv = lax.dot_general(low, ga, tn, preferred_element_type=F32)
        for j in range(SPAN):
            dwin_ref[j, 0, :, cols] = dk[j * toks : (j + 1) * toks].astype(BF16)
            dwin_ref[j, 1, :, cols] = dv[j * toks : (j + 1) * toks].astype(BF16)
        dkv_ref[0, :, cols] = dk[SPAN * toks :]
        dkv_ref[1, :, cols] = dv[SPAN * toks :]


def return_kernel(
    planes, fsdp,
    dwin, dkv, att, up_all,
    out_kv, out_w,
    g, share_in, y_in, c_in, z_in, att_all, w_out, w_in,
    load_sem, sh_send, sh_recv, y_send, y_recv, c_send, c_recv, z_send, z_recv,
    a_send, a_recv, b_send, b_recv, o_sem, w_send, w_recv,
):
    at = Place(planes, fsdp)
    toks = att.shape[0]
    rows = 2 * toks // CHUNKS
    width = att.shape[1]
    f = at.f
    mine = at.r * fsdp + f
    mates = at.mate * fsdp + f
    loads = [pltpu.make_async_copy(dwin.at[j], g.at[j], load_sem.at[j]) for j in range(SPAN)]
    for load in loads:
        load.start()
    own = pltpu.make_async_copy(att, att_all.at[mine], o_sem)
    own.start()
    at.barrier()

    def peers():
        for half in range(2):
            for df in range(fsdp):
                yield half, df, lax.rem(at.r + 2 * half, SPAN), lax.rem(f + df, fsdp)

    def a_copy(half, df, r, h):
        return remote(att, att_all.at[mine], a_send.at[half, df], a_recv.at[half, df], at.dev(at.p, r, h))

    def origin(half, df):
        return lax.rem(at.r + SPAN - 2 * half, SPAN) * fsdp + lax.rem(f + fsdp - df, fsdp)

    def b_copy(half, df):
        block = origin(half, df)
        src = att if half == 0 and df == 0 else att_all.at[block]
        return remote(src, att_all.at[block], b_send.at[half, df], b_recv.at[half, df], at.dev(at.p, at.mate, f))

    for half, df, r, h in peers():
        if half or df:
            a_copy(half, df, r, h).start()
    b_copy(0, 0).start()
    for load in loads:
        load.wait()

    def part(ref, c):
        return chunk_of(ref, c, rows)

    mate_across = lax.rem(at.mate + 2, SPAN)

    def sh_copy(c):
        return remote(part(g.at[mate_across], c), part(share_in, c), sh_send.at[c], sh_recv.at[c], at.dev(at.p, at.mate, f))

    def c_copy(c):
        return remote(part(g.at[at.mate], c), part(c_in, c), c_send.at[c], c_recv.at[c], at.dev(at.p, at.mate, f))

    def y_copy(c):
        return remote(part(g.at[at.across], c), part(y_in, c), y_send.at[c], y_recv.at[c], at.dev(at.p, at.across, f))

    def z_copy(c):
        return remote(part(g.at[at.r], c), part(z_in, c), z_send.at[c], z_recv.at[c], at.dev(at.p - 1, at.r, f))

    def first(c, _):
        sh_copy(c).start()
        c_copy(c).start()
        return 0

    lax.fori_loop(0, CHUNKS, first, 0)

    def where(c):
        per = CHUNKS // 2
        return lax.div(c, per), pl.ds(pl.multiple_of(lax.rem(c, per) * rows, rows), rows)

    def second(c, _):
        kv, span = where(c)
        sh_copy(c).wait_recv()
        g[at.across, kv, span] = (g[at.across, kv, span].astype(F32) + share_in[kv, span].astype(F32)).astype(BF16)
        y_copy(c).start()
        return 0

    lax.fori_loop(0, CHUNKS, second, 0)

    own.wait()
    for half, df, r, h in peers():
        if half or df:
            block = origin(half, df)
            remote(att_all.at[block], att_all.at[block], a_send.at[half, df], a_recv.at[half, df], at.dev(at.p, r, h)).wait_recv()
            b_copy(half, df).start()

    def third(c, _):
        kv, span = where(c)
        c_copy(c).wait_recv()
        y_copy(c).wait_recv()
        core_prev = at.core == 1
        y_prev = at.y == 1
        c_val = c_in[kv, span].astype(F32)
        y_val = y_in[kv, span].astype(F32)
        zero = jnp.zeros_like(c_val)
        prev = g[at.r, kv, span].astype(F32) + jnp.where(core_prev, c_val, zero) + jnp.where(y_prev, y_val, zero)
        g[at.r, kv, span] = prev.astype(BF16)
        dkv[kv, span] = dkv[kv, span] + jnp.where(core_prev, zero, c_val) + jnp.where(y_prev, zero, y_val)

        @pl.when(at.p > 0)
        def _():
            z_copy(c).start()

        return 0

    lax.fori_loop(0, CHUNKS, third, 0)

    for half, df, r, h in peers():
        block = lax.rem(at.mate + SPAN - 2 * half, SPAN) * fsdp + lax.rem(f + fsdp - df, fsdp)
        remote(att_all.at[block], att_all.at[block], b_send.at[half, df], b_recv.at[half, df], at.dev(at.p, at.mate, f)).wait_recv()
    tile = 256
    own_rows = out_w.shape[0]
    tn = (((0,), (0,)), ((), ()))
    tokens = SPAN * fsdp * toks
    lhs = up_all[...].reshape(tokens, up_all.shape[2])

    def mul(t, _):
        cols = pl.ds(pl.multiple_of(t * tile, tile), tile)
        value = lax.dot_general(lhs, att_all[:, :, cols].reshape(tokens, tile), tn, preferred_element_type=F32)
        out_w[:, cols] = jnp.zeros((own_rows, tile), F32)
        for q in range(planes):
            w_out[q, :, cols] = value[q * own_rows : (q + 1) * own_rows].astype(BF16)
        return 0

    lax.fori_loop(0, width // tile, mul, 0)

    def w_copy(dp):
        other = lax.rem(at.p + dp, planes)
        return remote(w_out.at[other], w_in.at[planes - dp], w_send.at[dp], w_recv.at[planes - dp], at.dev(other, at.r, f))

    for dp in range(1, planes):
        w_copy(dp).start()

    def fourth(c, _):
        kv, span = where(c)

        @pl.when(at.p < planes - 1)
        def _():
            z_copy(c).wait_recv()
            out_kv[kv, span] = (dkv[kv, span] + z_in[kv, span].astype(F32)).astype(BF16)

        @pl.when(at.p == planes - 1)
        def _():
            out_kv[kv, span] = dkv[kv, span].astype(BF16)

        sh_copy(c).wait_send()
        c_copy(c).wait_send()
        y_copy(c).wait_send()

        @pl.when(at.p > 0)
        def _():
            z_copy(c).wait_send()

        return 0

    lax.fori_loop(0, CHUNKS, fourth, 0)
    out_w[...] = w_out[at.p].astype(F32)
    for dp in range(1, planes):
        remote(w_in.at[dp], w_in.at[dp], w_send.at[dp], w_recv.at[dp], at.dev(lax.rem(at.p + dp, planes), at.r, f)).wait_recv()
        out_w[...] += w_in[dp].astype(F32)
    for dp in range(1, planes):
        w_copy(dp).wait_send()
    for half, df, r, h in peers():
        if half or df:
            a_copy(half, df, r, h).wait_send()
        b_copy(half, df).wait_send()


def shards(queries, keys_values, upstream, out_weight):
    seqs, toks, width = queries.shape
    ctx, fsdp = lax.axis_size("ctx"), lax.axis_size("fsdp")
    planes = ctx // SPAN
    model = upstream.shape[2]
    own_rows = model // (ctx * fsdp)
    group = SPAN * fsdp
    cols = planes * own_rows
    depth = out_weight.shape[0]
    kv = jnp.swapaxes(keys_values[0], 0, 1)
    up = upstream[0]
    up_cols = up.reshape(toks, planes, SPAN, fsdp, own_rows).transpose(2, 3, 0, 1, 4).reshape(group, toks, cols)
    dma = pltpu.SemaphoreType.DMA
    any_spec = pl.BlockSpec(memory_space=pl.ANY)
    vm = pl.BlockSpec(memory_space=pltpu.VMEM)
    chunk_rows = 2 * toks // CHUNKS
    win, grad_att, up_all = pl.pallas_call(
        functools.partial(gather_kernel, planes, fsdp),
        out_shape=(
            jax.ShapeDtypeStruct((SPAN, 2, toks, width), BF16),
            jax.ShapeDtypeStruct((toks, width), BF16),
            jax.ShapeDtypeStruct((group, toks, cols), BF16),
        ),
        in_specs=[any_spec, vm, vm, any_spec],
        out_specs=(any_spec, vm, vm),
        scratch_shapes=[
            pltpu.VMEM((depth, width), BF16),
            pltpu.VMEM((fsdp, toks, depth), BF16),
            pltpu.VMEM((fsdp, toks, width), BF16),
            pltpu.VMEM((fsdp, toks, width), BF16),
            pltpu.VMEM((chunk_rows, width), BF16),
            dma((CHUNKS,)), dma((CHUNKS,)), dma((CHUNKS,)), dma((CHUNKS,)),
            dma((SPAN, CHUNKS)), dma((CHUNKS,)), dma,
            dma((fsdp,)), dma((fsdp,)), dma((fsdp,)), dma((fsdp,)),
            dma((SPAN, fsdp)), dma((SPAN, fsdp)), dma,
        ],
        compiler_params=pltpu.CompilerParams(collective_id=0, has_side_effects=True),
        name="gather",
    )(kv, up, up_cols, out_weight)

    lane = 2 * HEAD_DIM
    flat = pl.BlockSpec((toks, lane), lambda h: (0, h))
    pair = pl.BlockSpec((2, toks, lane), lambda h: (0, 0, h))
    wide = pl.BlockSpec((SPAN, 2, toks, lane), lambda h: (0, 0, 0, h))
    dq, att, dkv, dwin = pl.pallas_call(
        attend_kernel,
        grid=(width // lane,),
        out_shape=(
            jax.ShapeDtypeStruct((toks, width), BF16),
            jax.ShapeDtypeStruct((toks, width), BF16),
            jax.ShapeDtypeStruct((2, toks, width), F32),
            jax.ShapeDtypeStruct((SPAN, 2, toks, width), BF16),
        ),
        in_specs=[flat, pair, wide, flat],
        out_specs=(flat, flat, pair, wide),
        name="attend",
    )(queries[0], kv, win, grad_att)

    out_kv, out_w = pl.pallas_call(
        functools.partial(return_kernel_wrapped, planes, fsdp),
        out_shape=(
            jax.ShapeDtypeStruct((2, toks, width), BF16),
            jax.ShapeDtypeStruct((own_rows, width), F32),
        ),
        in_specs=[any_spec, any_spec, vm, vm],
        out_specs=(vm, vm),
        scratch_shapes=[
            pltpu.VMEM((2, toks, width), F32),
            dma,
            pltpu.VMEM((SPAN, 2, toks, width), BF16),
            pltpu.VMEM((2, toks, width), BF16),
            pltpu.VMEM((2, toks, width), BF16),
            pltpu.VMEM((2, toks, width), BF16),
            pltpu.VMEM((2, toks, width), BF16),
            pltpu.VMEM((group, toks, width), BF16),
            pltpu.VMEM((planes, own_rows, width), BF16),
            pltpu.VMEM((planes, own_rows, width), BF16),
            dma((SPAN,)),
            dma((CHUNKS,)), dma((CHUNKS,)), dma((CHUNKS,)), dma((CHUNKS,)),
            dma((CHUNKS,)), dma((CHUNKS,)), dma((CHUNKS,)), dma((CHUNKS,)),
            dma((2, fsdp)), dma((2, fsdp)), dma((2, fsdp)), dma((2, fsdp)),
            dma, dma((planes,)), dma((planes,)),
        ],
        compiler_params=pltpu.CompilerParams(collective_id=1, has_side_effects=True),
        name="give_back",
    )(dwin, dkv, att, up_all)
    return dq[None], jnp.swapaxes(out_kv, 0, 1)[None], out_w


def return_kernel_wrapped(planes, fsdp, dwin, dkv_hbm, att, up_all, out_kv, out_w, dkv, dkv_sem, *rest):
    copy = pltpu.make_async_copy(dkv_hbm, dkv, dkv_sem)
    copy.start()
    copy.wait()
    return_kernel(planes, fsdp, dwin, dkv, att, up_all, out_kv, out_w, *rest)


def solution(mesh):
    return jax.shard_map(
        shards,
        mesh=mesh,
        in_specs=(
            P("fsdp", "ctx", None),
            P("fsdp", "ctx", None, None),
            P("fsdp", "ctx", None),
            P("fsdp", None),
        ),
        out_specs=(P("fsdp", "ctx", None), P("fsdp", "ctx", None, None), P(("ctx", "fsdp"), None)),
        check_vma=False,
    )
```

time: 429 us -> 150 us (0.35)
  waiting for transfers between devices: 277 us -> 0 us
  Pallas kernels: 0 us -> 136 us
  starting transfers between devices: 51.7 us -> 0 us
  local copies, waits for them, and re-layouts: 44.9 us -> 10 us
  matrix products: 32.7 us -> 0 us
  between operations: 13.9 us -> 0.66 us
  other arithmetic: 8.09 us -> 0 us
    reduce_scatter x2 -> x0, waiting for transfers between devices: 155 us -> none  [the longest x1 143 us: shards(): lax.psum_scatter(weight_term, 'ctx', scatter_dimension=0, tiled=True)]
    pallas_call x0 -> x3, Pallas kernels: none -> 136 us  [the longest x1 75.9 us: shards(): pl.pallas_call(functools.partial(return_kernel_wrapped, planes, fsdp), ou...]
    ppermute x8 -> x0, waiting for transfers between devices: 85.5 us -> none  [passed_along(): return lax.ppermute(x, axis, pairs)]
    ppermute x8 -> x0, starting transfers between devices: 51.4 us -> none  [passed_along(): return lax.ppermute(x, axis, pairs)]
    all_gather x1 -> x0, waiting for transfers between devices: 35.5 us -> none  [shards(): lax.all_gather(out_weight, 'fsdp', axis=0, tiled=True)]
    dot_general x7 -> x0, matrix products: 26.8 us -> none  [the longest x1 5.62 us: shards(): lax.dot_general(flat_upstream, flat_attended, (((0,), (0,)), ((), ())), p...]
    reshape x1, local copies, waits for them, and re-layouts: 13 us -> 1.01 us  [shards(): up.reshape(toks, planes, SPAN, fsdp, own_rows).transpose(2, 3, 0, 1, 4)]
    unnamed x31 -> x4, local copies, waits for them, and re-layouts: 18.8 us -> 9 us
  transfers between devices with their start and end apart: 11 -> 0, of which waited for: 10 -> 0; matrix products, arithmetic and copies ran while one was open for 11% -> 0% of each run, Pallas kernels for 0% -> 0%
where the time goes in v1:
time: 150 us; the launch traced here: 147 us
  Pallas kernels  136 us (91%)
  local copies, waits for them, and re-layouts  10 us (7%)
    pallas_call x1, Pallas kernels, shards(): pl.pallas_call(functools.partial(return_kernel_wrapped, planes, fsdp), ou...  75.9 us
    pallas_call x1, Pallas kernels, shards(): pl.pallas_call(functools.partial(gather_kernel, planes, fsdp), out_shape=...  44.7 us
    pallas_call x1, Pallas kernels, shards(): pl.pallas_call(attend_kernel, grid=(width // lane,), out_shape=(jax.Shape...  15.9 us
    unnamed x4, local copies, waits for them, and re-layouts  9 us

profile of v1, /device:TPU:0, one launch (start us, length us, event | category | flops | bytes accessed | tf_op | source)
XLA Modules:
  0.0 147.2 jit_solution(8308629561141939081)
XLA Ops:
  0.6 1.3 copy.11
  2.0 1.0 copy.13.up_cols
  3.0 2.5 %copy.16 = bf16[1,128,2,2048]{3,1,2,0:T(8,128)(2,1)} copy(bf16[1,128,2,2048]{3,2,1,0:T(2,128)(2,1)} %param.5) | data formatting | bytes 2097152 | tf_op args[1]
  5.5 44.7 %gather.1 = (bf16[4,2,128,2048]{3,2,1,0:T(8,128)(2,1)}, bf16[128,2048]{1,0:T(8,128)(2,1)}, bf16[8,128,256]{2,1,0:T(8,128)(2,1)}) custom-call(bf16[2,128,2048]{2,1,0:T(8,128)(2,1)} %bitcast.15, bf16[128,2048]{1,0:T(8,128)(2,1)} %bitcast.17, bf16[8,128,256]{2,1,0:T(8,128)(2,1)} %copy.13.up_cols, bf16[1024,2048]{1,0:T(8,128)(2,1)} %weight.1), custom_call_target="tpu_custom_call" | custom-call | tf_op jit(solution)/shard_map/gather/pallas_call | solution.py:466
  50.3 15.9 %attend.1 = (bf16[128,2048]{1,0:T(8,128)(2,1)}, bf16[128,2048]{1,0:T(8,128)(2,1)}, f32[2,128,2048]{2,1,0:T(8,128)}, bf16[4,2,128,2048]{3,2,1,0:T(8,128)(2,1)}) custom-call(bf16[128,2048]{1,0:T(8,128)(2,1)} %bitcast.21, bf16[2,128,2048]{2,1,0:T(8,128)(2,1)} %bitcast.16, bf16[4,2,128,2048]{3,2,1,0:T(8,128)(2,1)} %get-tuple-element.12.win_ref, ...), custom_call_target="tpu_custom_call" | custom-call | tf_op jit(solution)/shard_map/attend/pallas_call | solution.py:494
  66.2 75.9 %give_back.1 = (bf16[2,128,2048]{2,1,0:T(8,128)(2,1)}, f32[64,2048]{1,0:T(8,128)}) custom-call(bf16[4,2,128,2048]{3,2,1,0:T(8,128)(2,1)} %get-tuple-element.15.dwin, f32[2,128,2048]{2,1,0:T(8,128)} %get-tuple-element.16.dkv_hbm, bf16[128,2048]{1,0:T(8,128)(2,1)} %get-tuple-element.17.att, bf16[8,128,256]{2,1,0:T(8,128)(2,1)} %get-tuple-element.18.up_all), custom_call_target="tpu_custom_call" | custom-call | tf_op jit(solution)/shard_map/give_back/pallas_call | solution.py:508
  142.0 3.3 %copy.14 = bf16[1,128,2,2048]{3,2,1,0:T(2,128)(2,1)} copy(bf16[1,128,2,2048]{3,1,2,0:T(8,128)(2,1)} %bitcast.20) | data formatting | bytes 2097152
  145.3 1.9 %copy.18 = f32[64,2048]{1,0:T(8,128)} copy(f32[64,2048]{1,0:T(8,128)} %get-tuple-element.32) | data formatting | bytes 1048576
  (1 shorter events, 0.0 us)

commit v2 on v0

v2 whole, which is shorter than its diff:
```python
import functools

import jax
import jax.numpy as jnp
from jax import lax
from jax.experimental import pallas as pl
from jax.experimental.pallas import tpu as pltpu
from jax.sharding import PartitionSpec as P

HEADS = 16
HEAD_DIM = 128
SPAN = 4
WINDOW = 512
NEGATIVE = -1e30
CHUNKS = 8
AHEAD = 5
LAG = 2
F32 = jnp.float32
BF16 = jnp.bfloat16


class Place:
    def __init__(self, planes, fsdp):
        self.planes, self.fsdp = planes, fsdp
        me = lax.axis_index("ctx")
        self.f = lax.axis_index("fsdp")
        self.p = lax.div(me, SPAN)
        self.r = lax.rem(me, SPAN)
        self.core = lax.rem(self.r, 2)
        self.y = lax.div(self.r, 2)
        self.mate = self.r + 1 - 2 * self.core
        self.across = lax.rem(self.r + 2, SPAN)

    def dev(self, p, r, f):
        return {"ctx": p * SPAN + r, "fsdp": f}

    def members(self):
        for dr in range(SPAN):
            for df in range(self.fsdp):
                if dr or df:
                    yield lax.rem(self.r + dr, SPAN), lax.rem(self.f + df, self.fsdp), dr, df

    def barrier(self):
        sem = pltpu.get_barrier_semaphore()
        count = 0
        for r, f, _, _ in self.members():
            pl.semaphore_signal(sem, inc=1, device_id=self.dev(self.p, r, f), device_id_type=pl.DeviceIdType.MESH)
            count += 1
        for dp in range(1, self.planes):
            other = lax.rem(self.p + dp, self.planes)
            pl.semaphore_signal(sem, inc=1, device_id=self.dev(other, self.r, self.f), device_id_type=pl.DeviceIdType.MESH)
            count += 1
        pl.semaphore_wait(sem, count)


def remote(src, dst, send, recv, device):
    return pltpu.make_async_remote_copy(
        src_ref=src, dst_ref=dst, send_sem=send, recv_sem=recv, device_id=device, device_id_type=pl.DeviceIdType.MESH
    )


def chunk_cols(c, wide):
    return pl.ds(pl.multiple_of(c * wide, wide), wide)


def attend_head(q, ga, k, v, bias):
    inv_root = HEAD_DIM ** (-0.5)
    nt = (((1,), (1,)), ((), ()))
    tn = (((0,), (0,)), ((), ()))
    scores = lax.dot_general(q, k, nt, preferred_element_type=F32) * inv_root + bias
    lifted = jnp.exp(scores - jnp.max(scores, axis=-1, keepdims=True))
    prob = lifted * (1.0 / jnp.sum(lifted, axis=-1, keepdims=True))
    low = prob.astype(BF16)
    att = jnp.dot(low, v, preferred_element_type=F32).astype(BF16)
    products = lax.dot_general(ga, v, nt, preferred_element_type=F32)
    center = jnp.sum(ga.astype(F32) * att.astype(F32), axis=-1, keepdims=True)
    ds = (prob * (products - center)).astype(BF16)
    dq = (jnp.dot(ds, k, preferred_element_type=F32) * inv_root).astype(BF16)
    dk = lax.dot_general(ds, q, tn, preferred_element_type=F32) * inv_root
    dv = lax.dot_general(low, ga, tn, preferred_element_type=F32)
    return att, dq, dk, dv


def layer_kernel(
    planes, fsdp,
    q_ref, kv, up, up_cols, weight,
    dq_ref, out_kv, out_w,
    w_v, up_in, part_out, part_in, win, ga_ref, up_all, bias,
    g, dkv, share_in, y_in, c_in, z_in, att_all, w_out, w_in,
    fz_send, fy_send, fc_send, fs_send, slot_recv, w_sem, u_send, u_recv, q_send, q_recv, m_send, m_recv,
    sh_send, sh_recv, y_send, y_recv, c_send, c_recv, z_send, z_recv,
    a_send, a_recv, b_send, b_recv, r_send, r_recv,
):
    at = Place(planes, fsdp)
    toks = up.shape[0]
    depth = weight.shape[0]
    width = weight.shape[1]
    wide = width // CHUNKS
    f = at.f
    mine = at.r * fsdp + f
    mate_across = lax.rem(at.mate + 2, SPAN)
    mate = at.dev(at.p, at.mate, f)
    over = at.dev(at.p, at.across, f)
    w_copy = pltpu.make_async_copy(weight, w_v, w_sem)
    w_copy.start()

    @pl.when(at.p == 0)
    def _():
        win[at.r] = jnp.zeros(win.shape[1:], BF16)

    at.barrier()

    def cut(ref, c):
        return ref.at[:, :, chunk_cols(c, wide)]

    def up_copy(df):
        h = lax.rem(f + df, fsdp)
        return remote(
            up.at[:, pl.ds(pl.multiple_of(h * depth, 128), depth)], up_in.at[fsdp - df], u_send.at[df], u_recv.at[fsdp - df],
            at.dev(at.p, at.r, h),
        )

    def slot(j, c):
        return cut(win.at[j], c)

    def fz_copy(c):
        return remote(cut(kv, c), slot(at.r, c), fz_send.at[c], slot_recv.at[at.r, c], at.dev(at.p + 1, at.r, f))

    def fy_copy(c, src):
        return remote(src, slot(at.r, c), fy_send.at[c], slot_recv.at[at.r, c], over)

    def fc_copy(c, src):
        return remote(src, slot(at.r, c), fc_send.at[c], slot_recv.at[at.r, c], mate)

    def fs_copy(c):
        return remote(slot(at.across, c), slot(at.across, c), fs_send.at[c], slot_recv.at[at.across, c], mate)

    def arrived(j, c):
        remote(slot(j, c), slot(j, c), fz_send.at[c], slot_recv.at[j, c], mate).wait_recv()

    for df in range(1, fsdp):
        up_copy(df).start()

    def begin(c, _):
        @pl.when(at.p < planes - 1)
        def _():
            fz_copy(c).start()

        @pl.when(at.y == 0)
        def _():
            fy_copy(c, cut(kv, c)).start()

        @pl.when(at.core == 0)
        def _():
            fc_copy(c, cut(kv, c)).start()

        return 0

    lax.fori_loop(0, CHUNKS, begin, 0)

    row = lax.broadcasted_iota(jnp.int32, (toks, toks), 0)
    col = lax.broadcasted_iota(jnp.int32, (toks, toks), 1)
    for j in range(SPAN + 1):
        if j < SPAN:
            blocks = jnp.where(j < at.r, at.r - j, at.r - j + SPAN)
            limit = jnp.where(jnp.logical_and(at.p == 0, j >= at.r), 0, WINDOW)
        else:
            blocks, limit = 0, WINDOW
        distance = blocks * toks + row - col
        bias[:, j * toks : (j + 1) * toks] = jnp.where((distance >= 0) & (distance < limit), 0.0, NEGATIVE)

    w_copy.wait()
    tile = 512

    def product(lhs_of, put):
        def step(t, _):
            cols = chunk_cols(t, tile)
            put(cols, jnp.dot(lhs_of(), w_v[:, cols], preferred_element_type=F32))
            return 0

        lax.fori_loop(0, width // tile, step, 0)

    def part_copy(df):
        return remote(
            part_out.at[df], part_in.at[fsdp - df], q_send.at[df], q_recv.at[fsdp - df],
            at.dev(at.p, at.r, lax.rem(f + df, fsdp)),
        )

    for df in range(1, fsdp):
        remote(up_in.at[df], up_in.at[df], u_send.at[df], u_recv.at[df], at.dev(at.p, at.r, lax.rem(f + df, fsdp))).wait_recv()

        def put(cols, value, df=df):
            part_out[df, :, cols] = value.astype(BF16)

        product(lambda df=df: up_in[df], put)
        part_copy(df).start()

    def col_copy(r, h, dr, df):
        return remote(up_cols.at[r * fsdp + h], up_all.at[mine], m_send.at[dr, df], m_recv.at[dr, df], at.dev(at.p, r, h))

    for r, h, dr, df in at.members():
        col_copy(r, h, dr, df).start()
    up_all[mine] = up_cols[mine]

    def forward(c, _):
        @pl.when(at.p > 0)
        def _():
            arrived(at.r, c)

        @pl.when(at.y == 1)
        def _():
            fy_copy(c, slot(at.r, c)).start()

        @pl.when(at.core == 1)
        def _():
            fc_copy(c, slot(at.r, c)).start()

        arrived(at.across, c)
        fs_copy(c).start()
        return 0

    lax.fori_loop(0, AHEAD, forward, 0)
    own_depth = pl.ds(pl.multiple_of(f * depth, 128), depth)
    for df in range(1, fsdp):
        remote(part_in.at[df], part_in.at[df], q_send.at[df], q_recv.at[df], at.dev(at.p, at.r, lax.rem(f + df, fsdp))).wait_recv()

    def put_own(cols, value):
        for df in range(1, fsdp):
            value = value + part_in[df, :, cols].astype(F32)
        ga_ref[:, cols] = value.astype(BF16)

    product(lambda: up[:, own_depth], put_own)

    def peers():
        for half in range(2):
            for df in range(fsdp):
                yield half, df, lax.rem(at.r + 2 * half, SPAN), lax.rem(f + df, fsdp)

    def a_copy(half, df, r, h, view, c):
        return remote(view(att_all.at[mine]), view(att_all.at[mine]), a_send.at[half, df], a_recv.at[half, df, c], at.dev(at.p, r, h))

    def origin(half, df):
        return lax.rem(at.r + SPAN - 2 * half, SPAN) * fsdp + lax.rem(f + fsdp - df, fsdp)

    def b_copy(half, df, view, c):
        block = att_all.at[origin(half, df)]
        return remote(view(block), view(block), b_send.at[half, df], b_recv.at[half, df, c], mate)

    def whole(ref):
        return ref

    def sh_copy(c):
        return remote(cut(g.at[mate_across], c), cut(share_in, c), sh_send.at[c], sh_recv.at[c], mate)

    def c_copy(c):
        return remote(cut(g.at[at.mate], c), cut(c_in, c), c_send.at[c], c_recv.at[c], mate)

    def y_copy(c):
        return remote(cut(g.at[at.across], c), cut(y_in, c), y_send.at[c], y_recv.at[c], over)

    def z_copy(c):
        return remote(cut(g.at[at.r], c), cut(z_in, c), z_send.at[c], z_recv.at[c], at.dev(at.p - 1, at.r, f))

    def second(c, _):
        cols = chunk_cols(c, wide)
        sh_copy(c).wait_recv()
        g[at.across, :, :, cols] = (g[at.across, :, :, cols].astype(F32) + share_in[:, :, cols].astype(F32)).astype(BF16)
        y_copy(c).start()
        return 0

    def attend(c, _):
        @pl.when(c + AHEAD < CHUNKS)
        def _():
            forward(c + AHEAD, 0)

        arrived(at.mate, c)
        arrived(mate_across, c)
        for h in range(wide // HEAD_DIM):
            cols = pl.ds(pl.multiple_of(c * wide + h * HEAD_DIM, HEAD_DIM), HEAD_DIM)
            k = jnp.concatenate([win[j, 0, :, cols] for j in range(SPAN)] + [kv[0, :, cols]], axis=0)
            v = jnp.concatenate([win[j, 1, :, cols] for j in range(SPAN)] + [kv[1, :, cols]], axis=0)
            att, dq, dk, dv = attend_head(q_ref[:, cols], ga_ref[:, cols], k, v, bias[...])
            att_all[mine, :, cols] = att
            dq_ref[:, cols] = dq
            for j in range(SPAN):
                g[j, 0, :, cols] = dk[j * toks : (j + 1) * toks].astype(BF16)
                g[j, 1, :, cols] = dv[j * toks : (j + 1) * toks].astype(BF16)
            dkv[0, :, cols] = dk[SPAN * toks :]
            dkv[1, :, cols] = dv[SPAN * toks :]

        def view(ref):
            return ref.at[:, chunk_cols(c, wide)]

        for half, df, r, h in peers():
            if half or df:
                a_copy(half, df, r, h, view, c).start()
        b_copy(0, 0, view, c).start()
        sh_copy(c).start()
        c_copy(c).start()

        @pl.when(c >= LAG)
        def _():
            second(c - LAG, 0)

        return 0

    lax.fori_loop(0, CHUNKS, attend, 0)
    lax.fori_loop(CHUNKS - LAG, CHUNKS, second, 0)

    def third(c, _):
        cols = chunk_cols(c, wide)
        c_copy(c).wait_recv()
        y_copy(c).wait_recv()
        core_prev = at.core == 1
        y_prev = at.y == 1
        c_val = c_in[:, :, cols].astype(F32)
        y_val = y_in[:, :, cols].astype(F32)
        zero = jnp.zeros_like(c_val)
        prev = g[at.r, :, :, cols].astype(F32) + jnp.where(core_prev, c_val, zero) + jnp.where(y_prev, y_val, zero)
        g[at.r, :, :, cols] = prev.astype(BF16)
        dkv[:, :, cols] = dkv[:, :, cols] + jnp.where(core_prev, zero, c_val) + jnp.where(y_prev, zero, y_val)

        @pl.when(at.p > 0)
        def _():
            z_copy(c).start()

        return 0

    for r, h, dr, df in at.members():
        back = lax.rem(at.r + SPAN - dr, SPAN) * fsdp + lax.rem(f + fsdp - df, fsdp)
        remote(up_all.at[back], up_all.at[back], m_send.at[dr, df], m_recv.at[dr, df], at.dev(at.p, r, h)).wait_recv()
    own_rows = out_w.shape[0]
    tn = (((0,), (0,)), ((), ()))
    tokens = SPAN * fsdp * toks

    def r_copy(dp, view):
        other = lax.rem(at.p + dp, planes)
        return remote(
            view(w_out.at[other]), view(w_in.at[planes - dp]), r_send.at[dp], r_recv.at[planes - dp], at.dev(other, at.r, f)
        )

    def weigh(c, _):
        cols = chunk_cols(c, wide)

        def view(ref):
            return ref.at[:, cols]

        for half, df, r, h in peers():
            block = view(att_all.at[lax.rem(at.mate + SPAN - 2 * half, SPAN) * fsdp + lax.rem(f + fsdp - df, fsdp)])
            remote(block, block, b_send.at[half, df], b_recv.at[half, df, c], mate).wait_recv()
        lhs = up_all[...].reshape(tokens, up_all.shape[2])
        value = lax.dot_general(lhs, att_all[:, :, cols].reshape(tokens, wide), tn, preferred_element_type=F32)
        for n in range(planes):
            w_out[n, :, cols] = value[n * own_rows : (n + 1) * own_rows].astype(BF16)
        for dp in range(1, planes):
            r_copy(dp, view).start()
        return 0

    def relay(c, _):
        def view(ref):
            return ref.at[:, chunk_cols(c, wide)]

        for half, df, r, h in peers():
            if half or df:
                block = view(att_all.at[origin(half, df)])
                remote(block, block, a_send.at[half, df], a_recv.at[half, df, c], at.dev(at.p, r, h)).wait_recv()
                b_copy(half, df, view, c).start()

        @pl.when(c >= 1)
        def _():
            weigh(c - 1, 0)

        third(c, 0)
        return 0

    lax.fori_loop(0, CHUNKS, relay, 0)
    weigh(CHUNKS - 1, 0)

    def fourth(c, _):
        cols = chunk_cols(c, wide)

        @pl.when(at.p < planes - 1)
        def _():
            z_copy(c).wait_recv()
            out_kv[:, :, cols] = (dkv[:, :, cols] + z_in[:, :, cols].astype(F32)).astype(BF16)

        @pl.when(at.p == planes - 1)
        def _():
            out_kv[:, :, cols] = dkv[:, :, cols].astype(BF16)

        @pl.when(at.p < planes - 1)
        def _():
            fz_copy(c).wait_send()

        fy_copy(c, slot(at.r, c)).wait_send()
        fc_copy(c, slot(at.r, c)).wait_send()
        fs_copy(c).wait_send()
        sh_copy(c).wait_send()
        c_copy(c).wait_send()
        y_copy(c).wait_send()

        @pl.when(at.p > 0)
        def _():
            z_copy(c).wait_send()

        return 0

    lax.fori_loop(0, CHUNKS, fourth, 0)
    for df in range(1, fsdp):
        up_copy(df).wait_send()
        part_copy(df).wait_send()
    for r, h, dr, df in at.members():
        col_copy(r, h, dr, df).wait_send()
    for half, df, r, h in peers():
        if half or df:
            a_copy(half, df, r, h, whole, 0).wait_send()
        b_copy(half, df, whole, 0).wait_send()
    out_w[...] = w_out[at.p].astype(F32)
    for dp in range(1, planes):
        remote(w_in.at[dp], w_in.at[dp], r_send.at[dp], r_recv.at[dp], at.dev(lax.rem(at.p + dp, planes), at.r, f)).wait_recv()
        out_w[...] += w_in[dp].astype(F32)
    for dp in range(1, planes):
        r_copy(dp, whole).wait_send()


def shards(queries, keys_values, upstream, out_weight):
    seqs, toks, width = queries.shape
    ctx, fsdp = lax.axis_size("ctx"), lax.axis_size("fsdp")
    planes = ctx // SPAN
    model = upstream.shape[2]
    own_rows = model // (ctx * fsdp)
    group = SPAN * fsdp
    cols = planes * own_rows
    depth = out_weight.shape[0]
    kv = jnp.swapaxes(keys_values[0], 0, 1)
    up = upstream[0]
    up_cols = up.reshape(toks, planes, SPAN, fsdp, own_rows).transpose(2, 3, 0, 1, 4).reshape(group, toks, cols)
    dma = pltpu.SemaphoreType.DMA
    any_spec = pl.BlockSpec(memory_space=pl.ANY)
    vm = pl.BlockSpec(memory_space=pltpu.VMEM)
    block = (2, toks, width)
    line = dma((CHUNKS,))
    fan = dma((2, fsdp))
    spread = dma((2, fsdp, CHUNKS))
    dq, out_kv, out_w = pl.pallas_call(
        functools.partial(layer_kernel, planes, fsdp),
        out_shape=(
            jax.ShapeDtypeStruct((toks, width), BF16),
            jax.ShapeDtypeStruct(block, BF16),
            jax.ShapeDtypeStruct((own_rows, width), F32),
        ),
        in_specs=[vm, vm, vm, vm, any_spec],
        out_specs=(vm, vm, vm),
        scratch_shapes=[
            pltpu.VMEM((depth, width), BF16),
            pltpu.VMEM((fsdp, toks, depth), BF16),
            pltpu.VMEM((fsdp, toks, width), BF16),
            pltpu.VMEM((fsdp, toks, width), BF16),
            pltpu.VMEM((SPAN,) + block, BF16),
            pltpu.VMEM((toks, width), BF16),
            pltpu.VMEM((group, toks, cols), BF16),
            pltpu.VMEM((toks, (SPAN + 1) * toks), F32),
            pltpu.VMEM((SPAN,) + block, BF16),
            pltpu.VMEM(block, F32),
            pltpu.VMEM(block, BF16),
            pltpu.VMEM(block, BF16),
            pltpu.VMEM(block, BF16),
            pltpu.VMEM(block, BF16),
            pltpu.VMEM((group, toks, width), BF16),
            pltpu.VMEM((planes, own_rows, width), BF16),
            pltpu.VMEM((planes, own_rows, width), BF16),
            line, line, line, line, dma((SPAN, CHUNKS)), dma,
            dma((fsdp,)), dma((fsdp,)), dma((fsdp,)), dma((fsdp,)), dma((SPAN, fsdp)), dma((SPAN, fsdp)),
            line, line, line, line, line, line, line, line,
            fan, spread, fan, spread, dma((planes,)), dma((planes,)),
        ],
        compiler_params=pltpu.CompilerParams(collective_id=0, has_side_effects=True),
        name="layer",
    )(queries[0], kv, up, up_cols, out_weight)
    return dq[None], jnp.swapaxes(out_kv, 0, 1)[None], out_w


def solution(mesh):
    return jax.shard_map(
        shards,
        mesh=mesh,
        in_specs=(
            P("fsdp", "ctx", None),
            P("fsdp", "ctx", None, None),
            P("fsdp", "ctx", None),
            P("fsdp", None),
        ),
        out_specs=(P("fsdp", "ctx", None), P("fsdp", "ctx", None, None), P(("ctx", "fsdp"), None)),
        check_vma=False,
    )
```

time: 429 us -> 134 us (0.31)
  waiting for transfers between devices: 277 us -> 0 us
  Pallas kernels: 0 us -> 121 us
  starting transfers between devices: 51.7 us -> 0 us
  local copies, waits for them, and re-layouts: 44.9 us -> 11.9 us
  matrix products: 32.7 us -> 0 us
  between operations: 13.9 us -> 0.65 us
  other arithmetic: 8.09 us -> 0 us
    reduce_scatter x2 -> x0, waiting for transfers between devices: 155 us -> none  [the longest x1 143 us: shards(): lax.psum_scatter(weight_term, 'ctx', scatter_dimension=0, tiled=True)]
    pallas_call x0 -> x1, Pallas kernels: none -> 121 us  [shards(): pl.pallas_call(functools.partial(layer_kernel, planes, fsdp), out_shape=(...]
    ppermute x8 -> x0, waiting for transfers between devices: 85.5 us -> none  [passed_along(): return lax.ppermute(x, axis, pairs)]
    ppermute x8 -> x0, starting transfers between devices: 51.4 us -> none  [passed_along(): return lax.ppermute(x, axis, pairs)]
    all_gather x1 -> x0, waiting for transfers between devices: 35.5 us -> none  [shards(): lax.all_gather(out_weight, 'fsdp', axis=0, tiled=True)]
    dot_general x7 -> x0, matrix products: 26.8 us -> none  [the longest x1 5.62 us: shards(): lax.dot_general(flat_upstream, flat_attended, (((0,), (0,)), ((), ())), p...]
    reshape x1, local copies, waits for them, and re-layouts: 13 us -> 1.01 us  [shards(): up.reshape(toks, planes, SPAN, fsdp, own_rows).transpose(2, 3, 0, 1, 4)]
    unnamed x31 -> x5, local copies, waits for them, and re-layouts: 18.8 us -> 10.9 us
  transfers between devices with their start and end apart: 11 -> 0, of which waited for: 10 -> 0; matrix products, arithmetic and copies ran while one was open for 11% -> 0% of each run, Pallas kernels for 0% -> 0%
where the time goes in v2:
time: 134 us
  Pallas kernels  121 us (90%)
  local copies, waits for them, and re-layouts  11.9 us (9%)
    pallas_call x1, Pallas kernels, shards(): pl.pallas_call(functools.partial(layer_kernel, planes, fsdp), out_shape=(...  121 us
    unnamed x5, local copies, waits for them, and re-layouts  10.9 us

profile of v2, /device:TPU:0, one launch (start us, length us, event | category | flops | bytes accessed | tf_op | source)
XLA Modules:
  0.0 134.0 jit_solution(13412675077406915206)
XLA Ops:
  0.6 1.3 copy.11
  2.0 1.0 copy.13.up_cols
  3.0 2.5 %copy.16 = bf16[1,128,2,2048]{3,1,2,0:T(8,128)(2,1)} copy(bf16[1,128,2,2048]{3,2,1,0:T(2,128)(2,1)} %param.5) | data formatting | bytes 2097152 | tf_op args[1]
  5.5 121.4 %layer.1 = (bf16[128,2048]{1,0:T(8,128)(2,1)}, bf16[2,128,2048]{2,1,0:T(8,128)(2,1)}, f32[64,2048]{1,0:T(8,128)}) custom-call(bf16[128,2048]{1,0:T(8,128)(2,1)} %bitcast.21, bf16[2,128,2048]{2,1,0:T(8,128)(2,1)} %bitcast.15, bf16[128,2048]{1,0:T(8,128)(2,1)} %bitcast.18, bf16[8,128,256]{2,1,0:T(8,128)(2,1)} %copy.13.up_cols, bf16[1024,2048]{1,0:T(8,128)(2,1)} %weight.1), custom_call_target="tpu_custom_call" | custom-call | tf_op jit(solution)/shard_map/layer/pallas_call | solution.py:445
  127.0 3.3 %copy.14 = bf16[1,128,2,2048]{3,2,1,0:T(2,128)(2,1)} copy(bf16[1,128,2,2048]{3,1,2,0:T(8,128)(2,1)} %bitcast.19) | data formatting | bytes 2097152
  130.2 1.9 %copy.19 = bf16[1,128,2048]{2,1,0:T(8,128)(2,1)} copy(bf16[1,128,2048]{2,1,0:T(8,128)(2,1)} %bitcast.20) | data formatting | bytes 1048576
  132.1 1.9 %copy.20 = f32[64,2048]{1,0:T(8,128)} copy(f32[64,2048]{1,0:T(8,128)} %get-tuple-element.20) | data formatting | bytes 1048576
  (1 shorter events, 0.0 us)

commit v3 on v2

--- a/solution.py
+++ b/solution.py
@@ -15,6 +15,7 @@
 CHUNKS = 8
 AHEAD = 5
 LAG = 2
+DELAY = 4
 F32 = jnp.float32
 BF16 = jnp.bfloat16
 
@@ -268,6 +269,72 @@
         y_copy(c).start()
         return 0
 
+    def third(c, _):
+        cols = chunk_cols(c, wide)
+        c_copy(c).wait_recv()
+        y_copy(c).wait_recv()
+        core_prev = at.core == 1
+        y_prev = at.y == 1
+        c_val = c_in[:, :, cols].astype(F32)
+        y_val = y_in[:, :, cols].astype(F32)
+        zero = jnp.zeros_like(c_val)
+        prev = g[at.r, :, :, cols].astype(F32) + jnp.where(core_prev, c_val, zero) + jnp.where(y_prev, y_val, zero)
+        g[at.r, :, :, cols] = prev.astype(BF16)
+        dkv[:, :, cols] = dkv[:, :, cols] + jnp.where(core_prev, zero, c_val) + jnp.where(y_prev, zero, y_val)
+
+        @pl.when(at.p > 0)
+        def _():
+            z_copy(c).start()
+
+        return 0
+
+    for r, h, dr, df in at.members():
+        back = lax.rem(at.r + SPAN - dr, SPAN) * fsdp + lax.rem(f + fsdp - df, fsdp)
+        remote(up_all.at[back], up_all.at[back], m_send.at[dr, df], m_recv.at[dr, df], at.dev(at.p, r, h)).wait_recv()
+    own_rows = out_w.shape[0]
+    tn = (((0,), (0,)), ((), ()))
+    tokens = SPAN * fsdp * toks
+
+    def r_copy(dp, view):
+        other = lax.rem(at.p + dp, planes)
+        return remote(
+            view(w_out.at[other]), view(w_in.at[planes - dp]), r_send.at[dp], r_recv.at[planes - dp], at.dev(other, at.r, f)
+        )
+
+    def weigh(c, _):
+        cols = chunk_cols(c, wide)
+
+        def view(ref):
+            return ref.at[:, cols]
+
+        for half, df, r, h in peers():
+            block = view(att_all.at[lax.rem(at.mate + SPAN - 2 * half, SPAN) * fsdp + lax.rem(f + fsdp - df, fsdp)])
+            remote(block, block, b_send.at[half, df], b_recv.at[half, df, c], mate).wait_recv()
+        lhs = up_all[...].reshape(tokens, up_all.shape[2])
+        value = lax.dot_general(lhs, att_all[:, :, cols].reshape(tokens, wide), tn, preferred_element_type=F32)
+        for n in range(planes):
+            w_out[n, :, cols] = value[n * own_rows : (n + 1) * own_rows].astype(BF16)
+        for dp in range(1, planes):
+            r_copy(dp, view).start()
+        return 0
+
+    def relay(c, _):
+        def view(ref):
+            return ref.at[:, chunk_cols(c, wide)]
+
+        for half, df, r, h in peers():
+            if half or df:
+                block = view(att_all.at[origin(half, df)])
+                remote(block, block, a_send.at[half, df], a_recv.at[half, df, c], at.dev(at.p, r, h)).wait_recv()
+                b_copy(half, df, view, c).start()
+
+        @pl.when(c >= 1)
+        def _():
+            weigh(c - 1, 0)
+
+        third(c, 0)
+        return 0
+
     def attend(c, _):
         @pl.when(c + AHEAD < CHUNKS)
         def _():
@@ -302,78 +369,16 @@
         def _():
             second(c - LAG, 0)
 
+        @pl.when(c >= DELAY)
+        def _():
+            relay(c - DELAY, 0)
+
         return 0
 
     lax.fori_loop(0, CHUNKS, attend, 0)
     lax.fori_loop(CHUNKS - LAG, CHUNKS, second, 0)
 
-    def third(c, _):
-        cols = chunk_cols(c, wide)
-        c_copy(c).wait_recv()
-        y_copy(c).wait_recv()
-        core_prev = at.core == 1
-        y_prev = at.y == 1
-        c_val = c_in[:, :, cols].astype(F32)
-        y_val = y_in[:, :, cols].astype(F32)
-        zero = jnp.zeros_like(c_val)
-        prev = g[at.r, :, :, cols].astype(F32) + jnp.where(core_prev, c_val, zero) + jnp.where(y_prev, y_val, zero)
-        g[at.r, :, :, cols] = prev.astype(BF16)
-        dkv[:, :, cols] = dkv[:, :, cols] + jnp.where(core_prev, zero, c_val) + jnp.where(y_prev, zero, y_val)
-
-        @pl.when(at.p > 0)
-        def _():
-            z_copy(c).start()
-
-        return 0
-
-    for r, h, dr, df in at.members():
-        back = lax.rem(at.r + SPAN - dr, SPAN) * fsdp + lax.rem(f + fsdp - df, fsdp)
-        remote(up_all.at[back], up_all.at[back], m_send.at[dr, df], m_recv.at[dr, df], at.dev(at.p, r, h)).wait_recv()
-    own_rows = out_w.shape[0]
-    tn = (((0,), (0,)), ((), ()))
-    tokens = SPAN * fsdp * toks
-
-    def r_copy(dp, view):
-        other = lax.rem(at.p + dp, planes)
-        return remote(
-            view(w_out.at[other]), view(w_in.at[planes - dp]), r_send.at[dp], r_recv.at[planes - dp], at.dev(other, at.r, f)
-        )
-
-    def weigh(c, _):
-        cols = chunk_cols(c, wide)
-
-        def view(ref):
-            return ref.at[:, cols]
-
-        for half, df, r, h in peers():
-            block = view(att_all.at[lax.rem(at.mate + SPAN - 2 * half, SPAN) * fsdp + lax.rem(f + fsdp - df, fsdp)])
-            remote(block, block, b_send.at[half, df], b_recv.at[half, df, c], mate).wait_recv()
-        lhs = up_all[...].reshape(tokens, up_all.shape[2])
-        value = lax.dot_general(lhs, att_all[:, :, cols].reshape(tokens, wide), tn, preferred_element_type=F32)
-        for n in range(planes):
-            w_out[n, :, cols] = value[n * own_rows : (n + 1) * own_rows].astype(BF16)
-        for dp in range(1, planes):
-            r_copy(dp, view).start()
-        return 0
-
-    def relay(c, _):
-        def view(ref):
-            return ref.at[:, chunk_cols(c, wide)]
-
-        for half, df, r, h in peers():
-            if half or df:
-                block = view(att_all.at[origin(half, df)])
-                remote(block, block, a_send.at[half, df], a_recv.at[half, df, c], at.dev(at.p, r, h)).wait_recv()
-                b_copy(half, df, view, c).start()
-
-        @pl.when(c >= 1)
-        def _():
-            weigh(c - 1, 0)
-
-        third(c, 0)
-        return 0
-
-    lax.fori_loop(0, CHUNKS, relay, 0)
+    lax.fori_loop(CHUNKS - DELAY, CHUNKS, relay, 0)
     weigh(CHUNKS - 1, 0)
 
     def fourth(c, _):

time: 134 us -> 132 us (0.985)
  the two profiles are of different devices: /device:TPU:0 before, /device:TPU:4 now
where the time goes in v3:
time: 132 us
  Pallas kernels  120 us (91%)
  local copies, waits for them, and re-layouts  11.9 us (9%)
    pallas_call x1, Pallas kernels, shards(): pl.pallas_call(functools.partial(layer_kernel, planes, fsdp), out_shape=(...  120 us
    unnamed x5, local copies, waits for them, and re-layouts  10.9 us

profile of v3, /device:TPU:4, one launch (start us, length us, event | category | flops | bytes accessed | tf_op | source)
XLA Modules:
  0.0 132.1 jit_solution(8360269706733750843)
XLA Ops:
  0.6 1.3 copy.11
  2.0 1.0 copy.13.up_cols
  3.0 2.5 %copy.16 = bf16[1,128,2,2048]{3,1,2,0:T(8,128)(2,1)} copy(bf16[1,128,2,2048]{3,2,1,0:T(2,128)(2,1)} %param.5) | data formatting | bytes 2097152 | tf_op args[1]
  5.5 119.5 %layer.1 = (bf16[128,2048]{1,0:T(8,128)(2,1)}, bf16[2,128,2048]{2,1,0:T(8,128)(2,1)}, f32[64,2048]{1,0:T(8,128)}) custom-call(bf16[128,2048]{1,0:T(8,128)(2,1)} %bitcast.21, bf16[2,128,2048]{2,1,0:T(8,128)(2,1)} %bitcast.15, bf16[128,2048]{1,0:T(8,128)(2,1)} %bitcast.18, bf16[8,128,256]{2,1,0:T(8,128)(2,1)} %copy.13.up_cols, bf16[1024,2048]{1,0:T(8,128)(2,1)} %weight.1), custom_call_target="tpu_custom_call" | custom-call | tf_op jit(solution)/shard_map/layer/pallas_call | solution.py:450
  125.1 3.3 %copy.14 = bf16[1,128,2,2048]{3,2,1,0:T(2,128)(2,1)} copy(bf16[1,128,2,2048]{3,1,2,0:T(8,128)(2,1)} %bitcast.19) | data formatting | bytes 2097152
  128.3 1.9 %copy.19 = bf16[1,128,2048]{2,1,0:T(8,128)(2,1)} copy(bf16[1,128,2048]{2,1,0:T(8,128)(2,1)} %bitcast.20) | data formatting | bytes 1048576
  130.2 1.9 %copy.20 = f32[64,2048]{1,0:T(8,128)} copy(f32[64,2048]{1,0:T(8,128)} %get-tuple-element.20) | data formatting | bytes 1048576
  (1 shorter events, 0.0 us)
